TPU v7x, 512 devices: a whole 4x8x8 slice. The times are simulated.
512 devices in a mesh: ctx: 64 (over x, y, core), heads: 8 (over z).
Axes of the slice: x: 4, y: 8, z: 8, core: 2. Of those that a mesh axis runs over, the one named last changes fastest.
Arguments:
- ssm_input: bfloat16 [12288, 8192], P('ctx', 'heads'), may hold values from -36 to 36
- gate_input: bfloat16 [12288, 8192], P('ctx', 'heads'), may hold values from -6 to 6
- write_proj: bfloat16 [12288, 128], P('ctx'), may hold values from -0.5 to 0.5
- read_proj: bfloat16 [12288, 128], P('ctx'), may hold values from -0.5 to 0.5
- log_decay: float32 [12288, 128], P('ctx', 'heads'), may hold values from -0.75 to 0, as said below
- skip_gain: float32 [128], P('heads'), may hold values from 0.5 to 2
- norm_gain: float32 [8192], P('heads'), may hold values from 0.1 to 1.9
- query_rows: bfloat16 [12288, 4096], P('ctx', 'heads'), may hold values from -6 to 6
- key_rows: bfloat16 [12288, 1024], P('ctx', 'heads'), may hold values from -6 to 6
- value_rows: bfloat16 [12288, 1024], P('ctx', 'heads'), may hold values from -6 to 6
Outputs:
- ssm_out: bfloat16 [12288, 8192], P('ctx', 'heads')
- attn_out: bfloat16 [12288, 4096], P('ctx', 'heads')
Inputs may be any that keep to these rules, and one draw needn't show every extreme that they name: `log_decay`: negative everywhere.
All inputs are finite; a program needn't handle non-finite values.
Results may differ from a plain program's by a relative error of at most 0.0075.
Values may be sent and summed in bfloat16 or wider, within the bound.
No kernel may reach another device: no remote copies, remote signals or barrier semaphores. Data moves between devices by JAX's collectives and lax.ppermute only.
A program may use at most 128 MiB of HBM per device.

v0:
```python
import jax
import jax.numpy as jnp
from jax import lax
from jax.sharding import PartitionSpec as P

SSM_HEADS = 128
HEAD_P = 64
STATE = 128
QUERY_HEADS = 32
KV_HEADS = 8
HEAD_DIM = 128
SPAN = 64


def carried_in(part, axis, combine, identity):
    place = lax.axis_index(axis)
    gathered = jax.tree.map(lambda a: lax.all_gather(a, axis), part)
    state = jax.tree.map(lambda a, e: jnp.zeros_like(a) + jnp.asarray(e, a.dtype), part, identity)

    def one(step, state):
        return combine(
            state, jax.tree.map(lambda a: lax.dynamic_index_in_dim(a, step, 0, False), gathered)
        )

    return lax.fori_loop(0, place, one, state)


def chain_combine(earlier, later):
    return (earlier[0] * later[0], later[0][:, None, None] * earlier[1] + later[1])


def local_mixer(ssm_input, gate_input, write_proj, read_proj, log_decay, skip_gain, norm_gain):
    row_count, width_local = ssm_input.shape
    head_local = log_decay.shape[1]
    block_count = row_count // SPAN
    inputs_blk = ssm_input.reshape(block_count, SPAN, head_local, HEAD_P)
    inputs_float = inputs_blk.astype(jnp.float32)
    write_blk = write_proj.reshape(block_count, SPAN, STATE)
    read_blk = read_proj.reshape(block_count, SPAN, STATE)
    cum_decay = jnp.cumsum(log_decay.reshape(block_count, SPAN, head_local), axis=1)
    cum_heads = jnp.transpose(cum_decay, (0, 2, 1))
    causal = jnp.arange(SPAN)[:, None] >= jnp.arange(SPAN)[None, :]
    decay_gap = cum_heads[:, :, :, None] - cum_heads[:, :, None, :]
    decay_mask = jnp.where(causal, jnp.exp(jnp.where(causal, decay_gap, 0.0)), 0.0)
    intersection = jnp.einsum(
        "ctn,csn->cts", read_blk, write_blk, preferred_element_type=jnp.float32
    )
    mix_weights = intersection[:, None] * decay_mask
    y_local = jnp.einsum(
        "chts,cshp->cthp", mix_weights, inputs_float, precision=lax.Precision.HIGHEST
    )
    tail_decay = jnp.exp(cum_heads[:, :, -1:] - cum_heads)
    weighted_write = tail_decay[:, :, :, None] * write_blk[:, None].astype(jnp.float32)
    block_state = jnp.einsum(
        "cshp,chsn->chpn", inputs_float, weighted_write, precision=lax.Precision.HIGHEST
    )
    block_decay = jnp.exp(cum_heads[:, :, -1])

    def prefix_step(carry_in, block_item):
        return (chain_combine(carry_in, block_item), carry_in)

    start_pair = (
        jnp.ones((head_local,), jnp.float32),
        jnp.zeros((head_local, HEAD_P, STATE), jnp.float32),
    )
    device_pair, prefix_pair = lax.scan(prefix_step, start_pair, (block_decay, block_state))
    incoming = carried_in(device_pair, "ctx", chain_combine, start_pair)
    start_state = prefix_pair[0][:, :, None, None] * incoming[1][None] + prefix_pair[1]
    y_carry = (
        jnp.einsum(
            "ctn,chpn->cthp",
            read_blk.astype(jnp.float32),
            start_state,
            precision=lax.Precision.HIGHEST,
        )
        * jnp.exp(cum_decay)[:, :, :, None]
    )
    mixed_out = y_local + y_carry + skip_gain[None, None, :, None] * inputs_float
    gated = mixed_out.reshape(row_count, width_local) * jax.nn.silu(gate_input.astype(jnp.float32))
    square_total = lax.psum(jnp.sum(gated * gated, axis=1), "heads")
    row_scale = lax.rsqrt(square_total / (SSM_HEADS * HEAD_P) + 1e-05)
    return (gated * row_scale[:, None] * norm_gain[None, :]).astype(jnp.bfloat16)


def attend_block(
    state, query_block, query_positions, top_position, key_block, value_block, first_key
):
    scale_factor = 1.0 / HEAD_DIM**0.5
    key_count = key_block.shape[0]

    def compute(state_in):
        running_max, running_sum, running_acc = state_in
        scores = (
            jnp.einsum("gqd,ngd->gqn", query_block, key_block, preferred_element_type=jnp.float32)
            * scale_factor
        )
        key_positions = first_key + jnp.arange(key_count, dtype=jnp.int32)
        visible = key_positions[None, None, :] <= query_positions[None, :, None]
        block_max = jnp.max(jnp.where(visible, scores, -1e30), axis=2)
        new_max = jnp.maximum(running_max, block_max)
        weights = jnp.where(
            visible, jnp.exp(jnp.where(visible, scores - new_max[:, :, None], 0.0)), 0.0
        )
        rescale = jnp.exp(running_max - new_max)
        new_sum = rescale * running_sum + jnp.sum(weights, axis=2)
        new_acc = rescale[:, :, None] * running_acc + jnp.einsum(
            "gqn,ngd->gqd",
            weights.astype(jnp.bfloat16),
            value_block,
            preferred_element_type=jnp.float32,
        )
        return (new_max, new_sum, new_acc)

    return lax.cond(first_key > top_position, lambda state_in: state_in, compute, state)


def attention_local(query_rows, key_rows, value_rows):
    row_count = query_rows.shape[0]
    head_sets = key_rows.shape[1] // HEAD_DIM
    group_size = QUERY_HEADS // KV_HEADS
    own_index = lax.axis_index("ctx")
    query_stack = query_rows.reshape(row_count, head_sets, group_size, HEAD_DIM)
    query_stack = jnp.transpose(query_stack, (1, 0, 2, 3)).reshape(
        head_sets, row_count * group_size, HEAD_DIM
    )
    stacked_rows = jnp.arange(row_count * group_size, dtype=jnp.int32) // group_size
    own_positions = own_index * row_count + stacked_rows
    query_sets = [(query_stack, own_positions)]
    tops = [jnp.max(positions) for _, positions in query_sets]
    carries = tuple(
        (
            (
                jnp.full((head_sets, block.shape[1]), -1e30, jnp.float32),
                jnp.zeros((head_sets, block.shape[1]), jnp.float32),
                jnp.zeros((head_sets, block.shape[1], HEAD_DIM), jnp.float32),
            )
            for block, _ in query_sets
        )
    )
    key_piece = lax.all_gather(key_rows, "ctx", axis=0, tiled=True)
    value_piece = lax.all_gather(value_rows, "ctx", axis=0, tiled=True)
    piece_rows = key_piece.shape[0]
    key_blocks = key_piece.reshape(piece_rows // row_count, row_count, head_sets, HEAD_DIM)
    value_blocks = value_piece.reshape(piece_rows // row_count, row_count, head_sets, HEAD_DIM)
    offsets = row_count * jnp.arange(piece_rows // row_count, dtype=jnp.int32)

    def inner_step(states, block_item):
        key_block, value_block, first_key = block_item
        updated = tuple(
            (
                attend_block(
                    states[number],
                    query_sets[number][0],
                    query_sets[number][1],
                    tops[number],
                    key_block,
                    value_block,
                    first_key,
                )
                for number in range(len(query_sets))
            )
        )
        return (updated, None)

    result, _ = lax.scan(inner_step, carries, (key_blocks, value_blocks, offsets))
    finished = [(state[2] / state[1][:, :, None]).astype(jnp.bfloat16) for state in result]
    combined = finished[0]
    combined = combined.reshape(head_sets, row_count, group_size, HEAD_DIM)
    return jnp.transpose(combined, (1, 0, 2, 3)).reshape(
        row_count, head_sets * group_size * HEAD_DIM
    )


def body(
    ssm_input,
    gate_input,
    write_proj,
    read_proj,
    log_decay,
    skip_gain,
    norm_gain,
    query_rows,
    key_rows,
    value_rows,
):
    ssm_out = local_mixer(
        ssm_input, gate_input, write_proj, read_proj, log_decay, skip_gain, norm_gain
    )
    attn_out = attention_local(query_rows, key_rows, value_rows)
    return (ssm_out, attn_out)


def solution(mesh):
    in_specs = (
        P("ctx", "heads"),
        P("ctx", "heads"),
        P("ctx", None),
        P("ctx", None),
        P("ctx", "heads"),
        P("heads"),
        P("heads"),
        P("ctx", "heads"),
        P("ctx", "heads"),
        P("ctx", "heads"),
    )
    out_specs = (P("ctx", "heads"), P("ctx", "heads"))
    return jax.shard_map(body, mesh=mesh, in_specs=in_specs, out_specs=out_specs, check_vma=False)
```

profile of v0, /device:TPU:63, one launch (start us, length us, event | category | flops | bytes accessed | tf_op | source)
XLA Modules:
  0.0 625.4 jit_solution(15439639091845416310)
XLA Ops:
  13.1 6.8 %while.46 = (s32[]{:T(128)}, f32[16]{0:T(128)S(1)}, f32[16,64,128]{2,1,0:T(8,128)S(1)}, f32[3,16]{1,0:T(4,128)}, f32[3,16,64,128]{3,2,1,0:T(8,128)}, /*index=5*/...) while((s32[]{:T(128)}, f32[16]{0:T(128)S(1)}, ...), condition=%wide.region_2.3_spmd.clone, body=%wide.region_1.2_spmd.clone.sunk | while | flops 524323 | bytes 2622581 | solution.py:66
  23.0 124.2 %all-reduce = f32[1024]{0:T(1024)S(1)} all-reduce(f32[1024]{0:T(1024)S(1)} %dynamic-update-slice), channel_id=2, replica_groups=mesh['ctx'=64,'heads'=8] {'ctx'}, use_global_device_ids=true, to_apply=%add | all-reduce | flops 1024 | bytes 8192
  148.4 33.0 %all-gather.8.cloned.1.call-done = bf16[12288,128]{1,0:T(8,128)(2,1)} async-done(((bf16[192,128]{1,0:T(8,128)(2,1)}), bf16[12288,128]{1,0:T(8,128)(2,1)}) %all-gather.8.cloned.1.call-update) | async-done | bytes 3145744 | tf_op jit(solution)/shard_map/all_gather | solution.py:141
  181.4 336.1 %while.45 = (s32[]{:T(128)}, f32[1,768]{1,0:T(1,128)S(1)}, f32[1,768]{1,0:T(1,128)S(1)}, f32[1,768,128]{2,1,0:T(8,128)S(1)}, s32[64]{0:T(128)S(1)}, /*index=5*/s...) while((s32[]{:T(128)}, f32[1,768]{1,0:T(1,128)S(1)}, ...), condition=%wide.region_13.14_spmd.clone, body=%wide.region_8.13_spmd.clone.sunk | while | flops 77767872 | bytes 2938171 | solution.py:165
  183.4 3.3 conditional.3
  188.6 3.3 conditional.3
  199.1 3.3 conditional.3
  204.4 3.3 conditional.3
  209.6 3.3 conditional.3
  220.1 3.3 conditional.3
  251.6 3.3 conditional.3
  256.9 3.3 conditional.3
  262.1 3.3 conditional.3
  267.4 3.3 conditional.3
  272.7 3.3 conditional.3
  277.9 3.3 conditional.3
  283.2 3.3 conditional.3
  288.5 3.3 conditional.3
  293.7 3.3 conditional.3
  299.0 3.3 conditional.3
  309.5 3.3 conditional.3
  314.7 3.3 conditional.3
  518.6 78.0 %while.44 = (s32[]{:T(128)}, f32[16,64,128]{2,1,0:T(8,128)S(1)}, s32[]{:T(128)}, f32[64,16]{1,0:T(8,128)S(1)}, f32[64,16,64,128]{3,2,1,0:T(8,128)}, /*index=5*/s32[]{:T(128)}, s32[]{:T(128)}, s32[]{:T(128)}) while((s32[]{:T(128)}, f32[16,64,128]{2,1,0:T(8,128)S(1)}, s32[]{:T(128)}, f32[64,16]{1,0:T(8,128)S(1)}, f32[64,16,64,128]{3,2,1,0:T(8,128)}, ...), condition=%wide.region_4.5_spmd, body=%wide.region_3.4_spmd.sunk | while | flops 262149 | bytes 1573183 | solution.py:25
  603.3 14.5 %psum.7 = f32[192]{0:T(256)S(1)} all-reduce(f32[192]{0:T(256)S(1)} %multiply_reduce_fusion), channel_id=1, replica_groups=mesh['ctx'=64,'heads'=8] {'heads'}, use_global_device_ids=true, to_apply=%region_6.7 | all-reduce | flops 192 | bytes 1536 | tf_op jit(solution)/shard_map/psum | solution.py:80
  (952 shorter events, 503.4 us)
Async XLA Ops:
  7.2 141.0 %copy-start = (bf16[192,128]{1,0:T(8,128)(2,1)S(1)}, bf16[192,128]{1,0:T(8,128)(2,1)}, u32[]{:S(2)}) copy-start(bf16[192,128]{1,0:T(8,128)(2,1)} %param.21) | copy-start | bytes 147460
  7.2 4.2 copy-start.5
  7.2 141.2 %all-gather.6.cloned.1.call-start = ((), (), s32[]{:S(2)}) async-start(), calls=%async_computation | async-start | bytes 3194880 | tf_op jit(solution)/shard_map/all_gather | solution.py:140
  7.9 173.5 %all-gather.8.cloned.1.call-start = ((), (), s32[]{:S(2)}) async-start(), calls=%async_computation.1 | async-start | bytes 3194880 | tf_op jit(solution)/shard_map/all_gather | solution.py:141
  8.7 509.9 %all-gather.10.cloned.1.call-start = ((), (), s32[]{:S(2)}) async-start(), calls=%async_computation.2 | async-start | bytes 34078720 | tf_op jit(solution)/shard_map/all_gather | solution.py:17
  13.1 134.2 %copy-start.4 = (bf16[192,512]{1,0:T(8,128)(2,1)S(1)}, bf16[192,512]{1,0:T(8,128)(2,1)}, u32[]{:S(2)}) copy-start(bf16[192,512]{1,0:T(8,128)(2,1)} %param.25) | copy-start | bytes 589828
  20.0 0.8 copy-start.1
  518.6 78.1 %copy-start.2 = (f32[3,16,64,128]{3,2,1,0:T(8,128)S(1)}, f32[3,16,64,128]{3,2,1,0:T(8,128)}, u32[]{:S(2)}) copy-start(f32[3,16,64,128]{3,2,1,0:T(8,128)} %get-tuple-element.226) | copy-start | bytes 4718596
  518.6 78.1 %copy-start.7 = (f32[3,16]{1,0:T(4,128)S(1)}, f32[3,16]{1,0:T(4,128)}, u32[]{:S(2)}) copy-start(f32[3,16]{1,0:T(4,128)} %get-tuple-element.222) | copy-start | bytes 580
  596.7 2.5 copy-start.8
  602.0 1.0 copy-start.3
  602.0 15.8 %copy-start.6 = (f32[1024]{0:T(1024)S(1)}, f32[1024]{0:T(1024)}, u32[]{:S(2)}) copy-start(f32[1024]{0:T(1024)} %param.24) | copy-start | bytes 12292
Sparse Core Ops, SparseCore 0:
  11.4 85.3 all-gather.5
  100.1 81.2 all-gather.7
  184.8 144.7 all-gather.9
where the time goes:
time: 637 us; the launch traced here: 625 us
  matrix products  157 us (25%)
  blocking collectives  139 us (22%)
  other arithmetic  138 us (22%)
  loops' own time  88.4 us (14%)
  local copies, waits for them, and re-layouts  54.1 us (8%)
  waiting for transfers between devices  34.4 us (5%)
  between operations  14.7 us (2%)
    unnamed x1, blocking collectives  124 us
    dot_general x64, matrix products, compute(): jnp.einsum('gqn,ngd->gqd', weights.astype(jnp.bfloat16), value_block, pre...  83.3 us
    another operation x1, loops' own time, attention_local(): lax.scan(inner_step, carries, (key_blocks, value_blocks, offsets))  81.8 us
    add x66, other arithmetic, chain_combine(): later[0][:, None, None] * earlier[1] + later[1]  75.3 us
    dot_general x64, matrix products, compute(): jnp.einsum('gqd,ngd->gqn', query_block, key_block, preferred_element_type...  68.2 us
    dynamic_slice x64, local copies, waits for them, and re-layouts, attention_local(): lax.scan(inner_step, carries, (key_blocks, value_blocks, offsets))  41.2 us
    add x64, other arithmetic, compute(): key_positions = first_key + jnp.arange(key_count, dtype=jnp.int32)  39.9 us
    all_gather x1, waiting for transfers between devices, attention_local(): value_piece = lax.all_gather(value_rows, 'ctx', axis=0, tiled=True)  33 us
  transfers between devices with their start and end apart: 3, of which 1 were waited for; matrix products, arithmetic and copies ran while one was open for 42% of the time, Pallas kernels for 0%

commit v1 on v0

--- a/solution.py
+++ b/solution.py
@@ -10,6 +10,11 @@
 KV_HEADS = 8
 HEAD_DIM = 128
 SPAN = 64
+
+
+def all_by_exchange(shard, axis, dim):
+    sent = jnp.stack([shard] * lax.axis_size(axis))
+    return jnp.concatenate(lax.all_to_all(sent, axis, 0, 0), axis=dim)
 
 
 def carried_in(part, axis, combine, identity):
@@ -138,7 +143,7 @@
         )
     )
     key_piece = lax.all_gather(key_rows, "ctx", axis=0, tiled=True)
-    value_piece = lax.all_gather(value_rows, "ctx", axis=0, tiled=True)
+    value_piece = all_by_exchange(value_rows, "ctx", 0)
     piece_rows = key_piece.shape[0]
     key_blocks = key_piece.reshape(piece_rows // row_count, row_count, head_sets, HEAD_DIM)
     value_blocks = value_piece.reshape(piece_rows // row_count, row_count, head_sets, HEAD_DIM)

time: 637 us -> 681 us (1.069)
  blocking collectives: 139 us -> 209 us
  waiting for transfers between devices: 34.4 us -> 0.72 us
  starting transfers between devices: 0.11 us -> 10.9 us
    unnamed x1, blocking collectives: 124 us -> 190 us
    all_gather x1 -> x0, waiting for transfers between devices: 33 us -> none  [attention_local(): value_piece = lax.all_gather(value_rows, 'ctx', axis=0, tiled=True)]
    all_to_all x0 -> x1, starting transfers between devices: none -> 10.9 us  [all_by_exchange(): return jnp.concatenate(lax.all_to_all(sent, axis, 0, 0), axis=dim)]
  transfers between devices with their start and end apart: 3 -> 3, of which waited for: 1 -> 0; matrix products, arithmetic and copies ran while one was open for 42% -> 39% of each run, Pallas kernels for 0% -> 0%
where the time goes in v1:
time: 681 us; the launch traced here: 669 us
  blocking collectives  209 us (31%)
  matrix products  157 us (23%)
  other arithmetic  137 us (20%)
  loops' own time  88.7 us (13%)
  local copies, waits for them, and re-layouts  49.9 us (7%)
  between operations  15 us (2%)
  starting transfers between devices  10.9 us (2%)
    unnamed x1, blocking collectives  190 us
    dot_general x64, matrix products, compute(): jnp.einsum('gqn,ngd->gqd', weights.astype(jnp.bfloat16), value_block, pre...  83.2 us
    another operation x1, loops' own time, attention_local(): lax.scan(inner_step, carries, (key_blocks, value_blocks, offsets))  82.1 us
    add x66, other arithmetic, chain_combine(): later[0][:, None, None] * earlier[1] + later[1]  75.3 us
    dot_general x64, matrix products, compute(): jnp.einsum('gqd,ngd->gqn', query_block, key_block, preferred_element_type...  68.4 us
    add x64, other arithmetic, compute(): key_positions = first_key + jnp.arange(key_count, dtype=jnp.int32)  39.6 us
    dynamic_slice x64, local copies, waits for them, and re-layouts, attention_local(): lax.scan(inner_step, carries, (key_blocks, value_blocks, offsets))  38.1 us
    psum x1, blocking collectives, local_mixer(): square_total = lax.psum(jnp.sum(gated * gated, axis=1), 'heads')  19.3 us
  transfers between devices with their start and end apart: 3, of which 0 were waited for; matrix products, arithmetic and copies ran while one was open for 39% of the time, Pallas kernels for 0%

profile of v1, /device:TPU:63, one launch (start us, length us, event | category | flops | bytes accessed | tf_op | source)
XLA Modules:
  0.0 669.4 jit_solution(1923696052921374125)
XLA Ops:
  18.8 10.9 %all-to-all-start = ((bf16[64,192,128]{2,1,0:T(8,128)(2,1)}), bf16[64,192,128]{2,1,0:T(8,128)(2,1)}, u32[]{:S(2)}, u32[]{:S(2)}) async-start(bf16[64,192,128]{2,1,0:T(8,128)(2,1)} %stack.2), calls=%async_computation | async-start | bytes 6291456 | tf_op jit(solution)/shard_map/all_to_all | solution.py:17
  31.9 190.1 %all-reduce = f32[1024]{0:T(1024)S(1)} all-reduce(f32[1024]{0:T(1024)S(1)} %dynamic-update-slice), channel_id=2, replica_groups=mesh['ctx'=64,'heads'=8] {'ctx'}, use_global_device_ids=true, to_apply=%add | all-reduce | flops 1024 | bytes 8192
  223.2 333.1 %while.45 = (s32[]{:T(128)}, f32[1,768]{1,0:T(1,128)S(1)}, f32[1,768]{1,0:T(1,128)S(1)}, f32[1,768,128]{2,1,0:T(8,128)S(1)}, s32[64]{0:T(128)S(1)}, /*index=5*/s...) while((s32[]{:T(128)}, f32[1,768]{1,0:T(1,128)S(1)}, ...), condition=%wide.region_13.14_spmd.clone, body=%wide.region_8.13_spmd.clone.sunk | while | flops 77767872 | bytes 2938171 | solution.py:170
  230.3 3.3 conditional.3
  240.7 3.3 conditional.3
  251.1 3.3 conditional.3
  261.6 3.3 conditional.3
  277.2 3.3 conditional.3
  292.8 3.3 conditional.3
  308.4 3.3 conditional.3
  324.0 3.3 conditional.3
  339.6 3.3 conditional.3
  355.2 3.3 conditional.3
  386.5 3.3 conditional.3
  402.1 3.3 conditional.3
  417.7 3.3 conditional.3
  433.3 3.3 conditional.3
  448.9 3.3 conditional.3
  464.5 3.3 conditional.3
  480.1 3.3 conditional.3
  495.8 3.3 conditional.3
  511.4 3.3 conditional.3
  557.4 78.2 %while.44 = (s32[]{:T(128)}, f32[16,64,128]{2,1,0:T(8,128)S(1)}, s32[]{:T(128)}, f32[64,16]{1,0:T(8,128)S(1)}, f32[64,16,64,128]{3,2,1,0:T(8,128)}, /*index=5*/s32[]{:T(128)}, s32[]{:T(128)}, s32[]{:T(128)}) while((s32[]{:T(128)}, f32[16,64,128]{2,1,0:T(8,128)S(1)}, s32[]{:T(128)}, f32[64,16]{1,0:T(8,128)S(1)}, f32[64,16,64,128]{3,2,1,0:T(8,128)}, ...), condition=%wide.region_4.5_spmd, body=%wide.region_3.4_spmd.sunk | while | flops 262149 | bytes 1573183 | solution.py:30
  642.2 19.3 %psum.7 = f32[192]{0:T(256)S(1)} all-reduce(f32[192]{0:T(256)S(1)} %multiply_reduce_fusion), channel_id=1, replica_groups=mesh['ctx'=64,'heads'=8] {'heads'}, use_global_device_ids=true, to_apply=%region_6.7 | all-reduce | flops 192 | bytes 1536 | tf_op jit(solution)/shard_map/psum | solution.py:85
  (952 shorter events, 497.9 us)
Async XLA Ops:
  7.2 215.8 %copy-start = (bf16[192,128]{1,0:T(8,128)(2,1)S(1)}, bf16[192,128]{1,0:T(8,128)(2,1)}, u32[]{:S(2)}) copy-start(bf16[192,128]{1,0:T(8,128)(2,1)} %param.21) | copy-start | bytes 147460
  7.2 3.5 copy-start.5
  7.2 216.0 %all-gather.5.cloned.1.call-start = ((), (), s32[]{:S(2)}) async-start(), calls=%async_computation.1 | async-start | bytes 3194880 | tf_op jit(solution)/shard_map/all_gather | solution.py:145
  7.9 549.4 %all-gather.7.cloned.1.call-start = ((), (), s32[]{:S(2)}) async-start(), calls=%async_computation.2 | async-start | bytes 34078720 | tf_op jit(solution)/shard_map/all_gather | solution.py:22
  12.4 4.0 copy-start.6
  15.5 0.8 copy-start.1
  18.8 203.3 %copy-start.4 = (bf16[192,512]{1,0:T(8,128)(2,1)S(1)}, bf16[192,512]{1,0:T(8,128)(2,1)}, u32[]{:S(2)}) copy-start(bf16[192,512]{1,0:T(8,128)(2,1)} %param.25) | copy-start | bytes 589828
  18.8 204.3 %all-to-all-start = ((bf16[64,192,128]{2,1,0:T(8,128)(2,1)}), bf16[64,192,128]{2,1,0:T(8,128)(2,1)}, u32[]{:S(2)}, u32[]{:S(2)}) async-start(bf16[64,192,128]{2,1,0:T(8,128)(2,1)} %stack.2), calls=%async_computation | async-start | bytes 6291456 | tf_op jit(solution)/shard_map/all_to_all | solution.py:17
  557.4 78.2 %copy-start.2 = (f32[3,16,64,128]{3,2,1,0:T(8,128)S(1)}, f32[3,16,64,128]{3,2,1,0:T(8,128)}, u32[]{:S(2)}) copy-start(f32[3,16,64,128]{3,2,1,0:T(8,128)} %get-tuple-element.226) | copy-start | bytes 4718596
  635.6 2.5 copy-start.8
  640.9 1.0 copy-start.3
  640.9 20.6 %copy-start.7 = (f32[1024]{0:T(1024)S(1)}, f32[1024]{0:T(1024)}, u32[]{:S(2)}) copy-start(f32[1024]{0:T(1024)} %param.24) | copy-start | bytes 12292
Sparse Core Ops, SparseCore 0:
  11.4 96.7 all-gather.4
  111.6 145.4 all-gather.6
